TPU v7x, 32 devices: a whole 2x2x4 slice. The times are simulated.
32 devices in a mesh: grp: 4 (over x, core), seq: 8 (over z, y).
Axes of the slice: x: 2, y: 2, z: 4, core: 2. Of those that a mesh axis runs over, the one named last changes fastest.
Arguments:
- signal: float32 [64, 2048, 768], P('grp', 'seq'), may hold values from -36 to 36
- entry_gain: float32 [768], replicated
- entry_shift: float32 [768], replicated, may hold values from -3 to 3
- dilated_kernel: float32 [3, 768, 384], replicated
- middle_gain: float32 [384], replicated
- middle_shift: float32 [384], replicated, may hold values from -3 to 3
- pointwise_kernel: float32 [384, 768], replicated
- pointwise_bias: float32 [768], replicated, may hold values from -3 to 3
- lengths: int32 [64], replicated, may hold values from 128 to 1024, as said below
- assignment: int32 [4, 16], P('grp'), may hold values from 0 to 15, as said below
- cotangent: float32 [65536, 768], P(('grp', 'seq')), may hold values from -6 to 6
Outputs:
- activations: float32 [65536, 768], P(('grp', 'seq'))
- signal_gradient: float32 [64, 2048, 768], P('grp', 'seq')
- entry_gain_gradient: float32 [768], replicated
- entry_shift_gradient: float32 [768], replicated
- dilated_kernel_gradient: float32 [3, 768, 384], replicated
- middle_gain_gradient: float32 [384], replicated
- middle_shift_gradient: float32 [384], replicated
- pointwise_kernel_gradient: float32 [384, 768], replicated
- pointwise_bias_gradient: float32 [768], replicated
Inputs may be any that keep to these rules, and one draw needn't show every extreme that they name: `lengths`: valid rows of a window come first; some window is full with 1024 rows and some has exactly 128. `assignment`: each row lists the 16 windows of one group once.
All inputs are finite; a program needn't handle non-finite values.
Results may differ from a plain program's by a relative error of at most 0.0066.
Values may be sent and summed in bfloat16 or wider, within the bound.
No kernel may reach another device: no remote copies, remote signals or barrier semaphores. Data moves between devices by JAX's collectives and lax.ppermute only.
A program may use at most 128 MiB of HBM per device.

v0:
```python
import jax
import jax.numpy as jnp
from jax import lax
from jax.sharding import PartitionSpec as P

DILATION_STEP = 38
WINDOW_SPAN = 1024
HALF_WINDOW_ROWS = 512
EPSILON = 0.001


def from_partner(block, axis, bit):
    count = lax.axis_size(axis)
    route = []
    for low in range(count):
        high = low | 1 << bit
        if high != low and high < count:
            route += [(low, high), (high, low)]
    return lax.ppermute(block, axis, route)


def smooth(values):
    return jax.nn.gelu(values, approximate=True)


def moments(values, valid_mask, row_count):
    centre = lax.psum(jnp.sum(values * valid_mask, axis=(0, 1)), ("grp", "seq")) / row_count
    deviation = (values - centre) * valid_mask
    spread = lax.psum(jnp.sum(deviation * deviation, axis=(0, 1)), ("grp", "seq")) / row_count
    return (centre, lax.rsqrt(spread + EPSILON))


def extended(resident_rows, neighbour_border):
    position_count = resident_rows.shape[0]
    channel_width = resident_rows.shape[2]
    empty_row_block = jnp.zeros((position_count, DILATION_STEP, channel_width), resident_rows.dtype)
    bottom_portion = jnp.concatenate(
        [empty_row_block, resident_rows[:, :HALF_WINDOW_ROWS], neighbour_border[:, DILATION_STEP:]],
        axis=1,
    )
    top_portion = jnp.concatenate(
        [neighbour_border[:, :DILATION_STEP], resident_rows[:, HALF_WINDOW_ROWS:], empty_row_block],
        axis=1,
    )
    return jnp.stack([bottom_portion, top_portion], axis=1).reshape(
        2 * position_count, HALF_WINDOW_ROWS + 2 * DILATION_STEP, channel_width
    )


def per_device(
    signal,
    entry_gain,
    entry_shift,
    dilated_kernel,
    middle_gain,
    middle_shift,
    pointwise_kernel,
    pointwise_bias,
    lengths,
    assignment,
    cotangent,
):
    seq_count = lax.axis_size("seq")
    seq_place = lax.axis_index("seq")
    grp_place = lax.axis_index("grp")
    group_windows, segment, channel_width = signal.shape
    source_rows = segment // 2
    position_count = group_windows // seq_count
    bin_pairs = signal.reshape(group_windows, source_rows, 2, channel_width)
    first_bin = bin_pairs[:, :, 0]
    second_bin = bin_pairs[:, :, 1]
    take_first = first_bin >= second_bin
    group_lengths = lax.dynamic_slice_in_dim(lengths, grp_place * group_windows, group_windows)
    source_position = seq_place * source_rows + jnp.arange(source_rows, dtype=jnp.int32)
    source_valid = (source_position[None, :] < group_lengths[:, None]).astype(jnp.float32)[
        :, :, None
    ]
    pooled_low = (jnp.where(take_first, first_bin, second_bin) * source_valid).astype(jnp.bfloat16)
    window_order = assignment[0]
    upper_source = (seq_place >= seq_count // 2).astype(jnp.int32)
    targets = jnp.arange(seq_count, dtype=jnp.int32)
    slot_range = jnp.arange(position_count, dtype=jnp.int32)
    picked = window_order[
        (
            jnp.bitwise_xor(targets, upper_source)[:, None] * position_count + slot_range[None, :]
        ).reshape(-1)
    ]
    outgoing = jnp.take(pooled_low, picked, axis=0)
    arrived = lax.all_to_all(outgoing, "seq", split_axis=0, concat_axis=1, tiled=True)
    partner_place = jnp.bitwise_xor(seq_place, 1)
    own_windows = lax.dynamic_slice_in_dim(window_order, seq_place * position_count, position_count)
    partner_windows = lax.dynamic_slice_in_dim(
        window_order, partner_place * position_count, position_count
    )
    row_position = jnp.arange(WINDOW_SPAN, dtype=jnp.int32)
    limit_rows = jnp.where(
        row_position[None, :] < HALF_WINDOW_ROWS,
        jnp.take(group_lengths, own_windows)[:, None],
        jnp.take(group_lengths, partner_windows)[:, None],
    )
    valid_mask = (row_position[None, :] < limit_rows).astype(jnp.float32)[:, :, None]
    row_count = jnp.sum(lengths.astype(jnp.float32))
    pooled = arrived.astype(jnp.float32)
    entry_centre, entry_scale = moments(pooled, valid_mask, row_count)
    entry_norm = (pooled - entry_centre) * entry_scale
    entry_smooth, entry_back = jax.vjp(smooth, entry_norm * entry_gain + entry_shift)
    entry_activation = (entry_smooth * valid_mask).astype(jnp.bfloat16)
    kernel_low = dilated_kernel.astype(jnp.bfloat16)
    entry_border = from_partner(
        entry_activation[:, HALF_WINDOW_ROWS - DILATION_STEP : HALF_WINDOW_ROWS + DILATION_STEP],
        "seq",
        0,
    )
    entry_widened = extended(entry_activation, entry_border)
    dilated_out = jnp.zeros(
        (2 * position_count, HALF_WINDOW_ROWS, kernel_low.shape[2]), jnp.float32
    )
    for kernel_tap_index in range(3):
        displaced_rows = entry_widened[
            :,
            kernel_tap_index * DILATION_STEP : kernel_tap_index * DILATION_STEP + HALF_WINDOW_ROWS,
        ]
        dilated_out = dilated_out + jnp.einsum(
            "hrc,cf->hrf",
            displaced_rows,
            kernel_low[kernel_tap_index],
            preferred_element_type=jnp.float32,
        )
    dilated_out = dilated_out.reshape(position_count, WINDOW_SPAN, -1)
    middle_centre, middle_scale = moments(dilated_out, valid_mask, row_count)
    middle_norm = (dilated_out - middle_centre) * middle_scale
    middle_smooth, middle_back = jax.vjp(smooth, middle_norm * middle_gain + middle_shift)
    middle_act = (middle_smooth * valid_mask).astype(jnp.bfloat16)
    pointwise_low = pointwise_kernel.astype(jnp.bfloat16)
    mixed_out = jnp.einsum(
        "krf,fd->krd", middle_act, pointwise_low, preferred_element_type=jnp.float32
    )
    activations = (valid_mask * (pooled + mixed_out + pointwise_bias)).reshape(-1, channel_width)
    grad_block = cotangent.reshape(position_count, WINDOW_SPAN, channel_width) * valid_mask
    grad_mixed = grad_block.astype(jnp.bfloat16)
    bias_part = jnp.sum(grad_block, axis=(0, 1))
    pointwise_part = jnp.einsum(
        "krf,krd->fd", middle_act, grad_mixed, preferred_element_type=jnp.float32
    )
    grad_middle = jnp.einsum(
        "krd,fd->krf", grad_mixed, pointwise_low, preferred_element_type=jnp.float32
    )
    grad_middle_pre = middle_back(grad_middle * valid_mask)[0]
    middle_gain_part = jnp.sum(grad_middle_pre * middle_norm, axis=(0, 1))
    middle_shift_part = jnp.sum(grad_middle_pre, axis=(0, 1))
    (
        middle_gain_gradient,
        middle_shift_gradient,
        pointwise_kernel_gradient,
        pointwise_bias_gradient,
    ) = lax.psum((middle_gain_part, middle_shift_part, pointwise_part, bias_part), ("grp", "seq"))
    dilated_gradient = (
        middle_gain
        * middle_scale
        * (
            grad_middle_pre
            - (middle_shift_gradient + middle_norm * middle_gain_gradient) / row_count
        )
        * valid_mask
    )
    dilated_gradient = dilated_gradient.astype(jnp.bfloat16)
    border_gradient = from_partner(
        dilated_gradient[:, HALF_WINDOW_ROWS - DILATION_STEP : HALF_WINDOW_ROWS + DILATION_STEP],
        "seq",
        0,
    )
    grad_wide = extended(dilated_gradient, border_gradient)
    grad_halves = dilated_gradient.reshape(2 * position_count, HALF_WINDOW_ROWS, -1)
    kernel_pieces = []
    grad_entry = jnp.zeros((2 * position_count, HALF_WINDOW_ROWS, channel_width), jnp.float32)
    for kernel_tap_index in range(3):
        displaced_rows = entry_widened[
            :,
            kernel_tap_index * DILATION_STEP : kernel_tap_index * DILATION_STEP + HALF_WINDOW_ROWS,
        ]
        kernel_pieces.append(
            jnp.einsum(
                "hrc,hrf->cf", displaced_rows, grad_halves, preferred_element_type=jnp.float32
            )
        )
        backward_offset = (2 - kernel_tap_index) * DILATION_STEP
        grad_shifted = grad_wide[:, backward_offset : backward_offset + HALF_WINDOW_ROWS]
        grad_entry = grad_entry + jnp.einsum(
            "hrf,cf->hrc",
            grad_shifted,
            kernel_low[kernel_tap_index],
            preferred_element_type=jnp.float32,
        )
    kernel_part = jnp.stack(kernel_pieces)
    grad_entry = grad_entry.reshape(position_count, WINDOW_SPAN, channel_width)
    grad_entry_pre = entry_back(grad_entry * valid_mask)[0]
    entry_gain_part = jnp.sum(grad_entry_pre * entry_norm, axis=(0, 1))
    entry_shift_part = jnp.sum(grad_entry_pre, axis=(0, 1))
    entry_gain_gradient, entry_shift_gradient, dilated_kernel_gradient = lax.psum(
        (entry_gain_part, entry_shift_part, kernel_part), ("grp", "seq")
    )
    grad_pooled = (
        entry_gain
        * entry_scale
        * (grad_entry_pre - (entry_shift_gradient + entry_norm * entry_gain_gradient) / row_count)
        * valid_mask
        + grad_block
    )
    returned = lax.all_to_all(
        grad_pooled.astype(jnp.bfloat16), "seq", split_axis=1, concat_axis=0, tiled=True
    )
    inverse = (
        jnp.zeros((group_windows,), jnp.int32)
        .at[picked]
        .set(jnp.arange(group_windows, dtype=jnp.int32))
    )
    grad_source = jnp.take(returned, inverse, axis=0).astype(jnp.float32) * source_valid
    zero_part = jnp.zeros_like(grad_source)
    signal_gradient = jnp.stack(
        [
            jnp.where(take_first, grad_source, zero_part),
            jnp.where(take_first, zero_part, grad_source),
        ],
        axis=2,
    ).reshape(group_windows, segment, channel_width)
    return (
        activations,
        signal_gradient,
        entry_gain_gradient,
        entry_shift_gradient,
        dilated_kernel_gradient,
        middle_gain_gradient,
        middle_shift_gradient,
        pointwise_kernel_gradient,
        pointwise_bias_gradient,
    )


def solution(mesh):
    return jax.shard_map(
        per_device,
        mesh=mesh,
        in_specs=(
            P("grp", "seq", None),
            P(),
            P(),
            P(),
            P(),
            P(),
            P(),
            P(),
            P(),
            P("grp", None),
            P(("grp", "seq"), None),
        ),
        out_specs=(
            P(("grp", "seq"), None),
            P("grp", "seq", None),
            P(),
            P(),
            P(),
            P(),
            P(),
            P(),
            P(),
        ),
        check_vma=False,
    )
```

profile of v0, /device:TPU:0, one launch (start us, length us, event | category | flops | bytes accessed | tf_op | source)
XLA Modules:
  0.0 660.3 jit_solution(9878125855591612174)
XLA Ops:
  8.7 16.6 %copy.79 = f32[16,256,768]{2,0,1:T(8,128)} copy(f32[16,256,768]{2,1,0:T(8,128)} %param.15) | data formatting | bytes 25165824 | tf_op args[0]
  25.4 10.5 %fusion.86 = (f32[16,128,1,768]{3,0,2,1:T(8,128)}, f32[16,128,1,768]{3,0,2,1:T(8,128)}) fusion(f32[16,128,2,768]{3,0,2,1:T(8,128)} %bitcast.168), kind=kLoop, calls=%fused_computation.166 | loop fusion | bytes 25165824 | tf_op jit(solution)/shard_map/slice | solution.py:71
  36.1 11.7 %multiply_convert_fusion.1 = (bf16[16,128,768]{2,1,0:T(8,128)(2,1)}, pred[16,128,768]{2,1,0:T(8,128)(4,1)}) fusion(f32[16,128,1,768]{3,0,2,1:T(8,128)} %get-tuple-element.66, f32[16,128,1,768]{3,0,2,1:T(8,128)} %get-tuple-element.65, f32[16,128]{1,0:T(8,128)S(1)} %compare_convert_fusion.2), kind=kLoop, calls=%fused_computation.48 | loop fusion | flops 6291456 | bytes 17309696 | tf_op jit(solution)/shard_map/convert_element_type | solution.py:78
  47.8 2.6 gather_fusion.3
  50.4 2.0 broadcast_select_fusion.1
  52.4 7.4 %all-to-all-start = ((bf16[16,128,768]{2,1,0:T(8,128)(2,1)}), bf16[16,128,768]{2,1,0:T(8,128)(2,1)S(1)}, u32[]{:S(2)}, u32[]{:S(2)}) async-start(bf16[16,128,768]{2,1,0:T(8,128)(2,1)} %broadcast_select_fusion.1), calls=%async_computation | async-start | bytes 6291456 | tf_op jit(solution)/shard_map/all_to_all | solution.py:89
  61.7 3.7 convert_element_type.105
  66.3 5.2 multiply_convert_fusion.2
  71.5 3.5 fusion.38
  75.1 55.5 %all-to-all-done = bf16[16,128,768]{2,1,0:T(8,128)(2,1)S(1)} async-done(((bf16[16,128,768]{2,1,0:T(8,128)(2,1)}), bf16[16,128,768]{2,1,0:T(8,128)(2,1)S(1)}, u32[]{:S(2)}, u32[]{:S(2)}) %all-to-all-start) | async-done | bytes 3145760 | tf_op jit(solution)/shard_map/all_to_all | solution.py:89
  131.3 37.8 %psum.77 = f32[768]{0:T(1024)S(1)} all-reduce(f32[768]{0:T(1024)S(1)} %multiply_reduce_fusion.2), channel_id=1, replica_groups=mesh['grp'=4,'seq'=8] {'grp','seq'}, use_global_device_ids=true, to_apply=%region_1.4 | all-reduce | flops 768 | bytes 6144 | tf_op jit(solution)/shard_map/psum | solution.py:27
  170.8 41.7 %psum.78 = f32[768]{0:T(1024)S(1)} all-reduce(f32[768]{0:T(1024)S(1)} %multiply_reduce_fusion.1), channel_id=1, replica_groups=mesh['grp'=4,'seq'=8] {'grp','seq'}, use_global_device_ids=true, to_apply=%region_4.7 | all-reduce | flops 768 | bytes 6144 | tf_op jit(solution)/shard_map/psum | solution.py:29
  214.6 3.4 multiply_convert_fusion
  218.1 2.3 collective-permute-start
  220.6 4.9 collective-permute-done
  227.3 1.9 copy-done.10
  229.2 1.8 fusion.43
  231.0 1.8 fusion.51
  232.9 2.0 multiply_reduce_fusion.6
  234.9 38.2 %psum.79 = f32[384]{0:T(512)S(1)} all-reduce(f32[384]{0:T(512)S(1)} %get-tuple-element.86), channel_id=1, replica_groups=mesh['grp'=4,'seq'=8] {'grp','seq'}, use_global_device_ids=true, to_apply=%region_6.9 | all-reduce | flops 384 | bytes 3072 | tf_op jit(solution)/shard_map/psum | solution.py:27
  274.2 41.7 %psum.80 = f32[384]{0:T(512)S(1)} all-reduce(f32[384]{0:T(512)S(1)} %multiply_reduce_fusion.5), channel_id=1, replica_groups=mesh['grp'=4,'seq'=8] {'grp','seq'}, use_global_device_ids=true, to_apply=%region_8.11 | all-reduce | flops 384 | bytes 3072 | tf_op jit(solution)/shard_map/psum | solution.py:29
  316.6 6.1 fusion.81
  322.7 38.7 %all-reduce.1 = (f32[384]{0:T(512)S(1)}, f32[384]{0:T(512)S(1)}) all-reduce(f32[384]{0:T(512)S(1)} %get-tuple-element.50, f32[384]{0:T(512)S(1)} %get-tuple-element.49), channel_id=1, replica_groups=mesh['grp'=4,'seq'=8] {'grp','seq'}, use_global_device_ids=true, to_apply=%region_12.15 | all-reduce | flops 768 | bytes 6144 | tf_op jit(solution)/shard_map/psum | solution.py:156
  361.4 3.0 multiply_convert_fusion.5
  364.5 2.3 collective-permute-start.1
  367.0 2.7 collective-permute-done.1
  371.6 1.8 fusion.56
  373.5 1.8 fusion.58
  375.3 8.2 %fusion.80 = (f32[768]{0:T(1024)S(1)}, f32[768]{0:T(1024)S(1)}, f32[4,512,768]{2,1,0:T(8,128)}) fusion(f32[768]{0:T(1024)S(1)} %get-tuple-element.59, f32[4,512,768]{2,1,0:T(8,128)S(1)} %bitcast.163, f32[768]{0:T(1024)S(1)} %broadcast_divide_fusion, f32[768]{0:T(1024)S(1)} %copy-done.15, f32[768]{0:T(1024)S(1)} %copy-done.13, f32[4,512]{1,0:T(4,128)S(1)} %fusion.74, ...), kind=kOutput, calls=%fused_computation.162 | convolution fusion | flops 1253571072 | bytes 27359232 | tf_op jit(solution)/shard_map/hrf,cf->hrc/dot_general | solution.py:188
  383.5 41.3 %all-reduce = (f32[768]{0:T(1024)S(1)}, f32[768]{0:T(1024)S(1)}, f32[768]{0:T(1024)}) all-reduce(f32[768]{0:T(1024)S(1)} %get-tuple-element.48, f32[768]{0:T(1024)S(1)} %get-tuple-element.47, f32[768]{0:T(1024)S(1)} %get-tuple-element.68), channel_id=1, replica_groups=mesh['grp'=4,'seq'=8] {'grp','seq'}, use_global_device_ids=true, to_apply=%region_16.19 | all-reduce | flops 2304 | bytes 18432 | tf_op jit(solution)/shard_map/psum | solution.py:199
  424.8 11.1 %fusion.10 = bf16[2,1024,768]{2,1,0:T(8,128)(2,1)S(1)} fusion(f32[2,1024,768]{2,1,0:T(8,128)} %bitcast.164, f32[2,8,128,768]{3,2,1,0:T(8,128)} %copy-done.1, f32[]{:T(128)} %convert_reduce_fusion, f32[768]{0:T(1024)S(1)} %get-tuple-element.95, f32[768]{0:T(1024)S(1)} %get-tuple-element.96, f32[768]{0:T(1024)S(1)} %get-tuple-element.58, ...), kind=kLoop, calls=%fused_computation.21 | loop fusion | flops 51904512 | bytes 22049796 | tf_op jit(solution)/shard_map/convert_element_type | solution.py:210
  435.9 5.0 copy.86
  440.9 5.2 all-to-all-start.1
  446.2 4.3 fusion.60
  450.5 1.8 fusion.66
  452.3 1.8 fusion.63
  454.2 2.0 pad_maximum_fusion.2
  458.1 2.4 convolution_bitcast_fusion
  462.3 7.3 %fusion.19 = f32[2,1024,768]{2,1,0:T(8,128)} fusion(f32[2,8,128,768]{3,2,1,0:T(8,128)} %copy-done.1, f32[768]{0:T(1024)S(1)} %copy-done.17, f32[2,1024]{1,0:T(2,128)S(1)} %compare_convert_fusion.1, bf16[2,1024,384]{2,1,0:T(8,128)(2,1)S(1)} %copy-done.5, f32[384,768]{1,0:T(8,128)S(1)} %copy-done.7), kind=kOutput, calls=%fused_computation.36 | convolution fusion | flops 1212973056 | bytes 15346688 | tf_op jit(solution)/shard_map/krf,fd->krd/dot_general | solution.py:135
  469.6 68.6 %all-to-all-done.1 = bf16[2,1024,768]{2,0,1:T(2,128)(2,1)} async-done(((bf16[2,1024,768]{2,0,1:T(2,128)(2,1)}), bf16[2,1024,768]{2,0,1:T(2,128)(2,1)}, u32[]{:S(2)}, u32[]{:S(2)}) %all-to-all-start.1) | async-done | bytes 3145760 | tf_op jit(solution)/shard_map/all_to_all | solution.py:209
  538.2 2.3 copy.87
  540.7 2.4 gather_fusion.4
  543.1 5.3 select_bitcast_fusion.1
  548.4 9.2 %pad_maximum_fusion = f32[16,128,2,768]{3,1,0,2:T(8,128)} fusion(f32[16,128,1,768]{3,1,0,2:T(8,128)} %get-tuple-element.70, f32[16,128,1,768]{3,1,0,2:T(8,128)S(1)} %get-tuple-element.69), kind=kLoop, calls=%fused_computation.6 | loop fusion | flops 3145728 | bytes 25165824 | tf_op jit(solution)/shard_map/stack | solution.py:219
  557.6 16.5 %copy.89 = f32[16,128,2,768]{3,0,2,1:T(8,128)} copy(f32[16,128,2,768]{3,1,0,2:T(8,128)} %pad_maximum_fusion) | data formatting | bytes 25165824 | tf_op jit(solution)/shard_map/stack | solution.py:219
  574.0 16.9 %copy.94 = f32[16,256,768]{2,1,0:T(8,128)} copy(f32[16,256,768]{2,0,1:T(8,128)} %bitcast.169) | data formatting | bytes 25165824
  590.9 57.0 %all-reduce.5.cloned.1.call-done = (f32[3,768,384]{2,1,0:T(8,128)}, f32[384,768]{1,0:T(8,128)}) async-done(((f32[3,768,384]{2,1,0:T(8,128)}, f32[384,768]{1,0:T(8,128)}), (f32[3,768,384]{2,1,0:T(8,128)}, f32[384,768]{1,0:T(8,128)})) %all-reduce.5.cloned.1.call-update) | async-done | bytes 4718608 | tf_op jit(solution)/shard_map/psum | solution.py:199
  647.9 4.1 copy.127
  (128 shorter events, 19.6 us)
Async XLA Ops:
  25.4 10.5 %copy-start.22 = (s32[64]{0:T(128)S(1)}, s32[64]{0:T(128)}, u32[]{:S(2)}) copy-start(s32[64]{0:T(128)} %param.23) | copy-start | bytes 772
  52.4 7.5 %copy-start = (s32[1,16]{1,0:T(1,128)S(1)}, s32[1,16]{1,0:T(1,128)}, u32[]{:S(2)}) copy-start(s32[1,16]{1,0:T(1,128)} %param.24) | copy-start | bytes 196
  52.4 78.1 %all-to-all-start = ((bf16[16,128,768]{2,1,0:T(8,128)(2,1)}), bf16[16,128,768]{2,1,0:T(8,128)(2,1)S(1)}, u32[]{:S(2)}, u32[]{:S(2)}) async-start(bf16[16,128,768]{2,1,0:T(8,128)(2,1)} %broadcast_select_fusion.1), calls=%async_computation | async-start | bytes 6291456 | tf_op jit(solution)/shard_map/all_to_all | solution.py:89
  61.7 9.9 %slice-start.2 = ((s8[6291456]{0:T(1024)(128)(4,1)}), s8[4194304]{0:T(1024)(128)(4,1)S(1)}, s32[]{:S(2)}) async-start(s8[6291456]{0:T(1024)(128)(4,1)} %bitcast.165), calls=%async_computation.5 | async-start | bytes 8388608
  66.3 5.2 slice-start.3
  66.3 5.2 copy-start.6
  213.2 0.7 copy-start.13
  213.2 1.3 copy-start.15
  213.9 4.1 copy-start.1
  218.1 7.4 %collective-permute-start = (bf16[2,76,768]{2,1,0:T(8,128)(2,1)S(1)}, bf16[2,76,768]{2,1,0:T(8,128)(2,1)S(1)}, u32[]{:S(2)}, u32[]{:S(2)}) collective-permute-start(bf16[2,76,768]{2,1,0:T(8,128)(2,1)S(1)} %slice.103), channel_id=1, source_target_pairs={{0,1},{1,0},{2,3},{3,2},{4,5},{5,4},{6,7},{7,6},{8,9},{9,8},{10,11... | collective-permute-start | bytes 700424 | tf_op jit(solution)/shard_map/ppermute | solution.py:19
  227.0 2.1 copy-start.10
  227.3 5.6 copy-start.8
  234.9 81.1 %copy-start.14 = (f32[384]{0:T(512)S(1)}, f32[384]{0:T(512)}, u32[]{:S(2)}) copy-start(f32[384]{0:T(512)} %param.19) | copy-start | bytes 4612
  234.9 81.7 %copy-start.16 = (f32[384]{0:T(512)S(1)}, f32[384]{0:T(512)}, u32[]{:S(2)}) copy-start(f32[384]{0:T(512)} %param.20) | copy-start | bytes 4612
  361.4 3.1 copy-start.20
  361.4 3.1 copy-start.21
  364.4 2.4 copy-start.3
  364.5 5.2 collective-permute-start.1
  370.2 1.5 copy-start.11
  370.4 4.9 slice-start
  371.6 3.7 slice-start.1
  424.8 11.1 %copy-start.18 = (f32[768]{0:T(1024)}, f32[768]{0:T(1024)S(1)}, u32[]{:S(2)}) copy-start(f32[768]{0:T(1024)S(1)} %get-tuple-element.95) | copy-start | bytes 9220
  424.8 11.1 %copy-start.19 = (f32[768]{0:T(1024)}, f32[768]{0:T(1024)S(1)}, u32[]{:S(2)}) copy-start(f32[768]{0:T(1024)S(1)} %get-tuple-element.96) | copy-start | bytes 9220
  440.9 97.2 %all-to-all-start.1 = ((bf16[2,1024,768]{2,0,1:T(2,128)(2,1)}), bf16[2,1024,768]{2,0,1:T(2,128)(2,1)}, u32[]{:S(2)}, u32[]{:S(2)}) async-start(bf16[2,1024,768]{2,0,1:T(2,128)(2,1)} %copy.86), calls=%async_computation.1 | async-start | bytes 6291456 | tf_op jit(solution)/shard_map/all_to_all | solution.py:209
  446.1 201.8 %all-reduce.5.cloned.1.call-start = ((), (), s32[]{:S(2)}) async-start(), calls=%async_computation.2 | async-start | bytes 9437184 | tf_op jit(solution)/shard_map/psum | solution.py:199
  446.2 4.3 copy-start.4
  446.2 4.3 copy-start.9
  456.2 1.9 copy-start.2
  460.5 1.4 copy-start.5
  460.5 1.7 copy-start.7
  460.5 1.7 copy-start.17
  647.9 4.1 copy-start.12
Sparse Core Ops, SparseCore 0:
  460.7 187.1 all-reduce.4
where the time goes:
time: 668 us; the launch traced here: 660 us
  blocking collectives  239 us (36%)
  waiting for transfers between devices  189 us (28%)
  local copies, waits for them, and re-layouts  88.1 us (13%)
  other arithmetic  73 us (11%)
  matrix products  38.7 us (6%)
  starting transfers between devices  17.3 us (3%)
  between operations  15.1 us (2%)
    psum x2, blocking collectives, moments(): lax.psum(jnp.sum(deviation * deviation, axis=(0, 1)), ('grp', 'seq'))  83.4 us
    psum x2, blocking collectives, moments(): lax.psum(jnp.sum(values * valid_mask, axis=(0, 1)), ('grp', 'seq'))  76 us
    all_to_all x1, waiting for transfers between devices, per_device(): lax.all_to_all(grad_pooled.astype(jnp.bfloat16), 'seq', split_axis=1, con...  68.6 us
    psum x1, waiting for transfers between devices, per_device(): lax.psum((entry_gain_part, entry_shift_part, kernel_part), ('grp', 'seq'))  57 us
    all_to_all x1, waiting for transfers between devices, per_device(): lax.all_to_all(outgoing, 'seq', split_axis=0, concat_axis=1, tiled=True)  55.5 us
    unnamed x61, local copies, waits for them, and re-layouts  43.3 us
    psum x1, blocking collectives, per_device(): lax.psum((entry_gain_part, entry_shift_part, kernel_part), ('grp', 'seq'))  41.3 us
    psum x1, blocking collectives, per_device(): lax.psum((middle_gain_part, middle_shift_part, pointwise_part, bias_part)...  38.7 us
  transfers between devices with their start and end apart: 5, of which 5 were waited for; matrix products, arithmetic and copies ran while one was open for 14% of the time, Pallas kernels for 0%

commit v1 on v0

--- a/solution.py
+++ b/solution.py
@@ -197,7 +197,7 @@
     entry_gain_part = jnp.sum(grad_entry_pre * entry_norm, axis=(0, 1))
     entry_shift_part = jnp.sum(grad_entry_pre, axis=(0, 1))
     entry_gain_gradient, entry_shift_gradient, dilated_kernel_gradient = lax.psum(
-        (entry_gain_part, entry_shift_part, kernel_part), ("grp", "seq")
+        lax.psum((entry_gain_part, entry_shift_part, kernel_part), "seq"), "grp"
     )
     grad_pooled = (
         entry_gain

time: 668 us -> 865 us (1.29)
  waiting for transfers between devices: 189 us -> 398 us
  blocking collectives: 239 us -> 225 us
    psum x1 -> x3, waiting for transfers between devices: 57 us -> 335 us  [the longest x1 182 us: per_device(): lax.psum((entry_gain_part, entry_shift_part, kernel_part), 'seq')]
    all_to_all x1, waiting for transfers between devices: 68.6 us -> 0.01 us  [per_device(): lax.all_to_all(grad_pooled.astype(jnp.bfloat16), 'seq', split_axis=1, con...]
    psum x1 -> x2, blocking collectives: 41.3 us -> 26.7 us  [the longest x1 20.9 us: per_device(): lax.psum((entry_gain_part, entry_shift_part, kernel_part), 'seq')]
    unnamed x61 -> x63, local copies, waits for them, and re-layouts: 43.3 us -> 42.3 us
  transfers between devices with their start and end apart: 5 -> 7, of which waited for: 5 -> 6; matrix products, arithmetic and copies ran while one was open for 14% -> 10% of each run, Pallas kernels for 0% -> 0%
where the time goes in v1:
time: 865 us; the launch traced here: 857 us
  waiting for transfers between devices  398 us (46%)
  blocking collectives  225 us (26%)
  local copies, waits for them, and re-layouts  87 us (10%)
  other arithmetic  73.9 us (9%)
  matrix products  40.8 us (5%)
  starting transfers between devices  16.9 us (2%)
  between operations  14.9 us (2%)
    psum x1, waiting for transfers between devices, per_device(): lax.psum((entry_gain_part, entry_shift_part, kernel_part), 'seq')  182 us
    psum x2, blocking collectives, moments(): lax.psum(jnp.sum(deviation * deviation, axis=(0, 1)), ('grp', 'seq'))  83.5 us
    psum x1, waiting for transfers between devices, per_device(): lax.psum((middle_gain_part, middle_shift_part, pointwise_part, bias_part)...  76.8 us
    psum x1, waiting for transfers between devices, per_device(): lax.psum(lax.psum((entry_gain_part, entry_shift_part, kernel_part), 'seq'...  76.2 us
    psum x2, blocking collectives, moments(): lax.psum(jnp.sum(values * valid_mask, axis=(0, 1)), ('grp', 'seq'))  76 us
    all_to_all x1, waiting for transfers between devices, per_device(): lax.all_to_all(outgoing, 'seq', split_axis=0, concat_axis=1, tiled=True)  55.5 us
    unnamed x63, local copies, waits for them, and re-layouts  42.3 us
    psum x1, blocking collectives, per_device(): lax.psum((middle_gain_part, middle_shift_part, pointwise_part, bias_part)...  38.8 us
  transfers between devices with their start and end apart: 7, of which 6 were waited for; matrix products, arithmetic and copies ran while one was open for 10% of the time, Pallas kernels for 0%

profile of v1, /device:TPU:0, one launch (start us, length us, event | category | flops | bytes accessed | tf_op | source)
XLA Modules:
  0.0 856.6 jit_solution(8497132600829119011)
XLA Ops:
  8.7 16.6 %copy.79 = f32[16,256,768]{2,0,1:T(8,128)} copy(f32[16,256,768]{2,1,0:T(8,128)} %param.15) | data formatting | bytes 25165824 | tf_op args[0]
  25.4 10.6 %fusion.86 = (f32[16,128,1,768]{3,0,2,1:T(8,128)}, f32[16,128,1,768]{3,0,2,1:T(8,128)}) fusion(f32[16,128,2,768]{3,0,2,1:T(8,128)} %bitcast.168), kind=kLoop, calls=%fused_computation.166 | loop fusion | bytes 25165824 | tf_op jit(solution)/shard_map/slice | solution.py:71
  36.1 11.7 %multiply_convert_fusion.1 = (bf16[16,128,768]{2,1,0:T(8,128)(2,1)}, pred[16,128,768]{2,1,0:T(8,128)(4,1)}) fusion(f32[16,128,1,768]{3,0,2,1:T(8,128)} %get-tuple-element.66, f32[16,128,1,768]{3,0,2,1:T(8,128)} %get-tuple-element.65, f32[16,128]{1,0:T(8,128)S(1)} %compare_convert_fusion.2), kind=kLoop, calls=%fused_computation.48 | loop fusion | flops 6291456 | bytes 17309696 | tf_op jit(solution)/shard_map/convert_element_type | solution.py:78
  47.8 2.6 gather_fusion.3
  50.4 2.0 broadcast_select_fusion.1
  52.5 7.4 all-to-all-start
  61.7 3.5 convert_element_type.105
  66.3 5.2 multiply_convert_fusion.2
  71.6 3.5 fusion.38
  75.1 55.5 %all-to-all-done = bf16[16,128,768]{2,1,0:T(8,128)(2,1)S(1)} async-done(((bf16[16,128,768]{2,1,0:T(8,128)(2,1)}), bf16[16,128,768]{2,1,0:T(8,128)(2,1)S(1)}, u32[]{:S(2)}, u32[]{:S(2)}) %all-to-all-start) | async-done | bytes 3145760 | tf_op jit(solution)/shard_map/all_to_all | solution.py:89
  131.3 37.9 %psum.98 = f32[768]{0:T(1024)S(1)} all-reduce(f32[768]{0:T(1024)S(1)} %multiply_reduce_fusion.2), channel_id=1, replica_groups=mesh['grp'=4,'seq'=8] {'grp','seq'}, use_global_device_ids=true, to_apply=%region_1.4 | all-reduce | flops 768 | bytes 6144 | tf_op jit(solution)/shard_map/psum | solution.py:27
  170.9 41.7 %psum.99 = f32[768]{0:T(1024)S(1)} all-reduce(f32[768]{0:T(1024)S(1)} %multiply_reduce_fusion.1), channel_id=1, replica_groups=mesh['grp'=4,'seq'=8] {'grp','seq'}, use_global_device_ids=true, to_apply=%region_4.7 | all-reduce | flops 768 | bytes 6144 | tf_op jit(solution)/shard_map/psum | solution.py:29
  214.7 3.4 multiply_convert_fusion
  218.2 2.3 collective-permute-start
  220.8 4.9 collective-permute-done
  227.4 1.9 copy-done.9
  229.3 1.8 fusion.43
  233.0 2.0 multiply_reduce_fusion.6
  235.0 38.2 %psum.100 = f32[384]{0:T(512)S(1)} all-reduce(f32[384]{0:T(512)S(1)} %get-tuple-element.86), channel_id=1, replica_groups=mesh['grp'=4,'seq'=8] {'grp','seq'}, use_global_device_ids=true, to_apply=%region_6.9 | all-reduce | flops 384 | bytes 3072 | tf_op jit(solution)/shard_map/psum | solution.py:27
  274.4 41.8 %psum.101 = f32[384]{0:T(512)S(1)} all-reduce(f32[384]{0:T(512)S(1)} %multiply_reduce_fusion.5), channel_id=1, replica_groups=mesh['grp'=4,'seq'=8] {'grp','seq'}, use_global_device_ids=true, to_apply=%region_8.11 | all-reduce | flops 384 | bytes 3072 | tf_op jit(solution)/shard_map/psum | solution.py:29
  316.8 6.1 fusion.81
  322.9 38.8 %all-reduce = (f32[384]{0:T(512)S(1)}, f32[384]{0:T(512)S(1)}, f32[768]{0:T(1024)}) all-reduce(f32[384]{0:T(512)S(1)} %get-tuple-element.50, f32[384]{0:T(512)S(1)} %get-tuple-element.49, f32[768]{0:T(1024)S(1)} %get-tuple-element.68), channel_id=1, replica_groups=mesh['grp'=4,'seq'=8] {'grp','seq'}, use_global_device_ids=true, to_apply=%region_12.15 | all-reduce | flops 1536 | bytes 12288 | tf_op jit(solution)/shard_map/psum | solution.py:156
  361.7 3.4 multiply_convert_fusion.5
  365.2 2.8 fusion.66
  368.1 2.9 fusion.63
  370.9 2.6 collective-permute-start.1
  373.7 2.7 collective-permute-done.1
  380.2 1.8 fusion.58
  382.0 8.2 fusion.80
  390.2 20.9 %all-reduce.1 = (f32[768]{0:T(1024)S(1)}, f32[768]{0:T(1024)S(1)}) all-reduce(f32[768]{0:T(1024)S(1)} %get-tuple-element.48, f32[768]{0:T(1024)S(1)} %get-tuple-element.47), channel_id=1, replica_groups=mesh['grp'=4,'seq'=8] {'seq'}, use_global_device_ids=true, to_apply=%region_17.20 | all-reduce | flops 1536 | bytes 12288 | tf_op jit(solution)/shard_map/psum | solution.py:200
  411.1 5.8 all-reduce.2
  416.9 11.3 %fusion.10 = bf16[2,1024,768]{2,1,0:T(8,128)(2,1)S(1)} fusion(f32[2,1024,768]{2,1,0:T(8,128)} %bitcast.164, f32[2,8,128,768]{3,2,1,0:T(8,128)} %copy-done.1, f32[]{:T(128)} %convert_reduce_fusion, f32[768]{0:T(1024)S(1)} %get-tuple-element.95, f32[768]{0:T(1024)S(1)} %get-tuple-element.96, f32[768]{0:T(1024)S(1)} %get-tuple-element.58, ...), kind=kLoop, calls=%fused_computation.21 | loop fusion | flops 51904512 | bytes 22049796 | tf_op jit(solution)/shard_map/convert_element_type | solution.py:210
  428.3 4.8 copy.86
  433.1 4.4 all-to-all-start.1
  437.6 4.3 fusion.60
  442.0 2.0 pad_maximum_fusion.2
  446.0 2.4 convolution_bitcast_fusion
  449.2 182.1 %all-reduce.7.cloned.1.call-done = f32[3,768,384]{2,1,0:T(8,128)} async-done(((f32[3,768,384]{2,1,0:T(8,128)}), f32[3,768,384]{2,1,0:T(8,128)}) %all-reduce.7.cloned.1.call-update) | async-done | bytes 3538960 | tf_op jit(solution)/shard_map/psum | solution.py:200
  631.4 7.3 fusion.19
  638.7 2.3 copy.87
  641.2 2.4 gather_fusion.4
  643.6 5.3 select_bitcast_fusion.1
  648.9 9.2 %pad_maximum_fusion = f32[16,128,2,768]{3,1,0,2:T(8,128)} fusion(f32[16,128,1,768]{3,1,0,2:T(8,128)} %get-tuple-element.70, f32[16,128,1,768]{3,1,0,2:T(8,128)S(1)} %get-tuple-element.69), kind=kLoop, calls=%fused_computation.6 | loop fusion | flops 3145728 | bytes 25165824 | tf_op jit(solution)/shard_map/stack | solution.py:219
  658.1 16.4 %copy.89 = f32[16,128,2,768]{3,0,2,1:T(8,128)} copy(f32[16,128,2,768]{3,1,0,2:T(8,128)} %pad_maximum_fusion) | data formatting | bytes 25165824 | tf_op jit(solution)/shard_map/stack | solution.py:219
  674.5 16.9 %copy.94 = f32[16,256,768]{2,1,0:T(8,128)} copy(f32[16,256,768]{2,0,1:T(8,128)} %bitcast.169) | data formatting | bytes 25165824
  691.5 76.8 %all-reduce.11.cloned.1.call-done = f32[384,768]{1,0:T(8,128)} async-done(((f32[384,768]{1,0:T(8,128)}), f32[384,768]{1,0:T(8,128)}) %all-reduce.11.cloned.1.call-update) | async-done | bytes 1179664 | tf_op jit(solution)/shard_map/psum | solution.py:156
  768.3 76.2 %all-reduce.9.cloned.1.call-done = f32[3,768,384]{2,1,0:T(8,128)} async-done(((f32[3,768,384]{2,1,0:T(8,128)}), f32[3,768,384]{2,1,0:T(8,128)}) %all-reduce.9.cloned.1.call-update) | async-done | bytes 3538960 | tf_op jit(solution)/shard_map/psum | solution.py:199
  844.5 4.1 copy.128
  (137 shorter events, 22.6 us)
Async XLA Ops:
  25.4 10.6 %copy-start.23 = (s32[64]{0:T(128)S(1)}, s32[64]{0:T(128)}, u32[]{:S(2)}) copy-start(s32[64]{0:T(128)} %param.23) | copy-start | bytes 772
  52.5 7.5 copy-start
  52.5 78.1 %all-to-all-start = ((bf16[16,128,768]{2,1,0:T(8,128)(2,1)}), bf16[16,128,768]{2,1,0:T(8,128)(2,1)S(1)}, u32[]{:S(2)}, u32[]{:S(2)}) async-start(bf16[16,128,768]{2,1,0:T(8,128)(2,1)} %broadcast_select_fusion.1), calls=%async_computation | async-start | bytes 6291456 | tf_op jit(solution)/shard_map/all_to_all | solution.py:89
  61.7 9.9 %slice-start.2 = ((s8[6291456]{0:T(1024)(128)(4,1)}), s8[4194304]{0:T(1024)(128)(4,1)S(1)}, s32[]{:S(2)}) async-start(s8[6291456]{0:T(1024)(128)(4,1)} %bitcast.165), calls=%async_computation.7 | async-start | bytes 8388608
  66.3 5.3 slice-start.3
  66.3 5.3 copy-start.5
  213.3 0.7 copy-start.14
  213.3 1.4 copy-start.16
  214.0 4.2 copy-start.1
  218.2 7.4 collective-permute-start
  227.2 2.1 copy-start.9
  227.4 5.5 copy-start.7
  235.0 81.1 %copy-start.15 = (f32[384]{0:T(512)S(1)}, f32[384]{0:T(512)}, u32[]{:S(2)}) copy-start(f32[384]{0:T(512)} %param.19) | copy-start | bytes 4612
  235.0 81.8 %copy-start.17 = (f32[384]{0:T(512)S(1)}, f32[384]{0:T(512)}, u32[]{:S(2)}) copy-start(f32[384]{0:T(512)} %param.20) | copy-start | bytes 4612
  361.7 3.4 copy-start.21
  361.7 3.5 copy-start.22
  361.7 3.5 copy-start.8
  365.2 8.3 copy-start.3
  370.9 5.4 collective-permute-start.1
  376.9 1.5 copy-start.10
  377.1 4.9 slice-start
  378.3 3.7 slice-start.1
  416.9 11.3 %copy-start.19 = (f32[768]{0:T(1024)}, f32[768]{0:T(1024)S(1)}, u32[]{:S(2)}) copy-start(f32[768]{0:T(1024)S(1)} %get-tuple-element.95) | copy-start | bytes 9220
  416.9 11.3 %copy-start.20 = (f32[768]{0:T(1024)}, f32[768]{0:T(1024)S(1)}, u32[]{:S(2)}) copy-start(f32[768]{0:T(1024)S(1)} %get-tuple-element.96) | copy-start | bytes 9220
  433.1 205.6 %all-to-all-start.1 = ((bf16[2,1024,768]{2,0,1:T(2,128)(2,1)}), bf16[2,1024,768]{2,0,1:T(2,128)(2,1)}, u32[]{:S(2)}, u32[]{:S(2)}) async-start(bf16[2,1024,768]{2,0,1:T(2,128)(2,1)} %copy.86), calls=%async_computation.1 | async-start | bytes 6291456 | tf_op jit(solution)/shard_map/all_to_all | solution.py:209
  437.6 193.7 %all-reduce.7.cloned.1.call-start = ((), (), s32[]{:S(2)}) async-start(), calls=%async_computation.2 | async-start | bytes 7077888 | tf_op jit(solution)/shard_map/psum | solution.py:200
  437.6 4.3 copy-start.11
  437.6 4.3 copy-start.12
  444.0 324.2 %all-reduce.11.cloned.1.call-start = ((), (), s32[]{:S(2)}) async-start(), calls=%async_computation.4 | async-start | bytes 2359296 | tf_op jit(solution)/shard_map/psum | solution.py:156
  444.1 1.9 copy-start.2
  448.4 182.9 %copy-start.4 = (bf16[2,1024,384]{2,1,0:T(8,128)(2,1)S(1)}, bf16[2,1024,384]{2,1,0:T(8,128)(2,1)}, u32[]{:S(2)}) copy-start(bf16[2,1024,384]{2,1,0:T(8,128)(2,1)} %get-tuple-element.71) | copy-start | bytes 4718596
  448.4 182.9 %copy-start.6 = (f32[384,768]{1,0:T(8,128)S(1)}, f32[384,768]{1,0:T(8,128)}, u32[]{:S(2)}) copy-start(f32[384,768]{1,0:T(8,128)} %param.21) | copy-start | bytes 3538948
  448.4 183.0 %copy-start.18 = (f32[768]{0:T(1024)S(1)}, f32[768]{0:T(1024)}, u32[]{:S(2)}) copy-start(f32[768]{0:T(1024)} %param.22) | copy-start | bytes 9220
  448.5 396.0 %all-reduce.9.cloned.1.call-start = ((), (), s32[]{:S(2)}) async-start(), calls=%async_computation.3 | async-start | bytes 7077888 | tf_op jit(solution)/shard_map/psum | solution.py:199
  844.5 4.1 copy-start.13
Sparse Core Ops, SparseCore 0:
  444.2 187.1 all-reduce.6
  638.2 130.0 all-reduce.10
  770.7 73.7 all-reduce.8
